TPU v7x, 512 devices: a whole 4x8x8 slice. The times are simulated.
512 devices in a mesh: section: 4 (over x), sub: 32 (over z_lo, y), rng: 4 (over z_hi, core).
Axes of the slice: x: 4, y: 8, z: 8 (z_hi: 2, z_lo: 4; z = z_hi * 4 + z_lo), core: 2. Of those that a mesh axis runs over, the one named last changes fastest.
Arguments:
- echoes: bfloat16 [2, 32, 24, 16384], P(None, 'sub', 'section', 'rng'), may hold values from -6 to 6
- chirp: bfloat16 [2, 2048], replicated, may hold values from -0.25 to 0.25
- steer: bfloat16 [2, 32, 128, 24], P(None, 'sub'), may hold values from -2 to 2
- pulse_order: int32 [32, 24], P('sub'), may hold values from 0 to 23, each once within a row
- band_coef: bfloat16 [5, 32, 2, 2, 128, 16], P(None, 'sub'), may hold values from -2.5 to 2.5
- band_start: int32 [5, 32, 2, 128], P(None, 'sub'), may hold values from 0 to 112
- band_width: int32 [5, 32, 2, 128], P(None, 'sub'), may hold values from 1 to 16
Outputs:
- image: bfloat16 [2, 4096, 4, 4096], P(None, 'sub', 'rng', 'section')
Inputs may be any that keep to these rules, and one draw needn't show every extreme that they name: `pulse_order`: each row is a permutation of the 24 aperture positions.
All inputs are finite; a program needn't handle non-finite values.
Results may differ from a plain program's by a relative error of at most 0.0085.
Values may be sent and summed in bfloat16 or wider, within the bound.
A program may use at most 64 MiB of HBM per device.

v0:
```python
import jax
import jax.numpy as jnp
from jax import lax
from jax.sharding import PartitionSpec as P

CBLK = 128


def from_behind(value, axis, by):
    size = lax.axis_size(axis)
    pairs = [(i, i + by) for i in range(size) if 0 <= i + by < size]
    return lax.ppermute(value, axis, pairs)


def from_partner(block, axis, stride):
    count = lax.axis_size(axis)
    route = []
    for low in range(count):
        high = low | 1 << stride
        if high != low and high < count:
            route += [(low, high), (high, low)]
    return lax.ppermute(block, axis, route)


def band_matrix(coef_side, start_side, width_side):
    beam_count = coef_side.shape[1]
    tap_count = coef_side.shape[2]
    column = jnp.arange(beam_count, dtype=jnp.int32)
    offset = column[None, :] - start_side[:, None]
    taps = jnp.arange(tap_count, dtype=jnp.int32)
    hits = (offset[None, :, :] == taps[:, None, None]) & (
        taps[:, None, None] < width_side[None, :, None]
    )
    selector = hits.astype(jnp.bfloat16)
    return jnp.einsum(
        "sqt,tqc->sqc", coef_side, selector, preferred_element_type=jnp.float32
    ).astype(jnp.bfloat16)


def merge_level(own, partner_image, coef_level, start_level, width_level):
    self_matrix = band_matrix(coef_level[0], start_level[0], width_level[0])
    cross_matrix = band_matrix(coef_level[1], start_level[1], width_level[1])
    upper_rows = jnp.concatenate(
        [self_matrix[0], -self_matrix[1], cross_matrix[0], -cross_matrix[1]], axis=1
    )
    lower_rows = jnp.concatenate(
        [self_matrix[1], self_matrix[0], cross_matrix[1], cross_matrix[0]], axis=1
    )
    operator = jnp.concatenate([upper_rows, lower_rows], axis=0)
    stacked = jnp.concatenate([own[0], own[1], partner_image[0], partner_image[1]], axis=0)
    merged = jnp.dot(operator, stacked, preferred_element_type=jnp.float32)
    return merged.reshape(2, own.shape[1], own.shape[2]).astype(jnp.bfloat16)


def lag_tables(chirp, extra_blocks):
    tap_count = chirp.shape[1]
    padded = jnp.concatenate(
        [jnp.zeros((2, CBLK), jnp.bfloat16), chirp, jnp.zeros((2, 2 * CBLK), jnp.bfloat16)], axis=1
    )
    total_len = tap_count + 3 * CBLK
    tiled = jnp.tile(padded, (1, CBLK))[:, : CBLK * (total_len - 1)]
    shifted = tiled.reshape(2, CBLK, total_len - 1)[:, :, CBLK : CBLK + (extra_blocks + 1) * CBLK]
    shifted = shifted.reshape(2, CBLK, extra_blocks + 1, CBLK)
    return jnp.transpose(shifted, (0, 2, 3, 1))


def compress(signal, chirp):
    pulse_count = signal.shape[1]
    range_count = signal.shape[2]
    tap_count = chirp.shape[1]
    next_rim = from_behind(signal[:, :, :tap_count], "rng", -1)
    extended = jnp.concatenate([signal, next_rim], axis=2)
    block_count = range_count // CBLK
    extra_blocks = tap_count // CBLK
    blocks = extended.reshape(2, pulse_count, block_count + extra_blocks, CBLK)
    blocks = jnp.transpose(blocks, (1, 2, 0, 3)).reshape(
        pulse_count, block_count + extra_blocks, 2 * CBLK
    )
    parts_table = lag_tables(chirp, extra_blocks)
    chirp_real = parts_table[0]
    chirp_imag = parts_table[1]
    upper_rows = jnp.concatenate([chirp_real, -chirp_imag], axis=2)
    lower_rows = jnp.concatenate([chirp_imag, chirp_real], axis=2)
    tables = jnp.concatenate([upper_rows, lower_rows], axis=1)

    def add_piece(lag, accumulated):
        window = lax.dynamic_slice_in_dim(blocks, lag, block_count, 1)
        table = lax.dynamic_index_in_dim(tables, lag, 0, keepdims=False)
        return accumulated + jnp.einsum(
            "pbi,io->pbo", window, table, preferred_element_type=jnp.float32
        )

    accumulated = lax.fori_loop(
        0, extra_blocks + 1, add_piece, jnp.zeros((pulse_count, block_count, 2 * CBLK), jnp.float32)
    )
    accumulated = accumulated.reshape(pulse_count, block_count, 2, CBLK)
    return (
        jnp.transpose(accumulated, (2, 0, 1, 3))
        .reshape(2, pulse_count, range_count)
        .astype(jnp.bfloat16)
    )


def on_device(echoes, chirp, steer, pulse_order, band_coef, band_start, band_width):
    compressed = compress(echoes[:, 0], chirp)
    pulse_rows = lax.all_to_all(compressed, "section", split_axis=2, concat_axis=1, tiled=True)
    position_count = pulse_order.shape[1]
    positions = jnp.arange(position_count, dtype=jnp.int32)
    selector = (positions[:, None] == pulse_order[0][None, :]).astype(jnp.bfloat16)
    weights = jnp.einsum(
        "sqj,jk->sqk", steer[:, 0], selector, preferred_element_type=jnp.float32
    ).astype(jnp.bfloat16)
    forming = jnp.concatenate(
        [
            jnp.concatenate([weights[0], -weights[1]], axis=1),
            jnp.concatenate([weights[1], weights[0]], axis=1),
        ],
        axis=0,
    )
    stacked_rows = jnp.concatenate([pulse_rows[0], pulse_rows[1]], axis=0)
    beam_count = weights.shape[1]
    level_image = (
        jnp.dot(forming, stacked_rows, preferred_element_type=jnp.float32)
        .reshape(2, beam_count, pulse_rows.shape[2])
        .astype(jnp.bfloat16)
    )
    bit_count = lax.axis_size("sub").bit_length() - 1
    coef_all = band_coef[:, 0]
    start_all = band_start[:, 0]
    width_all = band_width[:, 0]
    section_count = coef_all.shape[0]
    for level in range(section_count):
        partner_image = from_partner(level_image, "sub", level % bit_count)
        level_image = merge_level(
            level_image, partner_image, coef_all[level], start_all[level], width_all[level]
        )
    return level_image[:, :, None, :]


def solution(mesh):
    return jax.shard_map(
        on_device,
        mesh=mesh,
        in_specs=(
            P(None, "sub", "section", "rng"),
            P(),
            P(None, "sub", None, None),
            P("sub", None),
            P(None, "sub", None, None, None, None),
            P(None, "sub", None, None),
            P(None, "sub", None, None),
        ),
        out_specs=P(None, "sub", "rng", "section"),
        check_vma=False,
    )
```

profile of v0, /device:TPU:6, one launch (start us, length us, event | category | flops | bytes accessed | tf_op | source)
XLA Modules:
  0.0 177.9 jit_solution(6251457165325808575)
XLA Ops:
  0.0 1.5 slice.437
  1.5 1.3 collective-permute-start
  2.8 0.7 maximum_maximum_fusion.1
  3.6 1.3 copy.173
  4.9 0.9 slice.438
  5.9 2.1 %reshape.582 = bf16[622336]{0:T(1024)(128)(2,1)S(1)} reshape(bf16[2,311168]{1,0:T(2,128)(2,1)S(1)} %slice.438) | data formatting | bytes 2489344
  8.0 2.2 %reshape.578 = bf16[2,128,2431]{2,1,0:T(8,128)(2,1)S(1)} reshape(bf16[622336]{0:T(1024)(128)(2,1)S(1)} %reshape.582) | data formatting | bytes 2489344 | tf_op jit(solution)/shard_map/reshape | solution.py:62
  10.2 1.1 slice.439
  11.2 1.7 copy.133
  13.1 0.9 fusion.186
  14.0 0.5 slice_bitcast_fusion.33
  14.5 0.6 slice_bitcast_fusion.32
  15.1 0.6 fusion.198
  16.6 0.6 fusion.195
  17.4 0.5 fusion.13
  17.8 0.7 fusion.208
  18.6 0.6 fusion.196
  19.4 0.6 slice_bitcast_fusion.12
  20.3 0.5 fusion.10
  20.9 0.6 fusion.193
  21.7 0.5 fusion.11
  22.1 0.7 fusion.206
  22.8 0.6 fusion.194
  23.8 0.5 fusion.8
  24.4 0.7 fusion.191
  25.6 0.7 fusion.204
  26.4 0.6 fusion.192
  27.0 0.8 iota_subtract_fusion.6
  27.8 1.4 maximum_maximum_fusion
  29.2 1.1 maximum_bitcast_fusion
  30.4 4.0 %while.14 = (s32[]{:T(128)}, f32[6,32,256]{2,1,0:T(8,128)S(1)}, bf16[6,48,256]{2,1,0:T(8,128)(2,1)S(1)}, bf16[17,256,256]{2,1,0:T(8,128)(2,1)S(1)}, s32[]{:T(128)}, /*index=5*/s32[]{:T(128)}) while((s32[]{:T(128)}, f32[6,32,256]{2,1,0:T(8,128)S(1)}, bf16[6,48,256]{2,1,0:T(8,128)(2,1)S(1)}, bf16[17,256,256]{2,1,0:T(8,128)(2,1)S(1)}, ...), condition=%wide.region_1.2_spmd.clone, body=%wide.region_0.1_spmd.clone.sunk | while | flops 25264132 | bytes 623695 | solution.py:93
  34.4 1.4 copy.140
  35.8 4.2 %reshape.584 = bf16[4,2,6144]{2,1,0:T(2,128)(2,1)} reshape(bf16[4096,2,6]{2,1,0:T(2,128)(2,1)S(1)} %bitcast.228) | data formatting | bytes 196608
  40.0 9.1 %all-to-all-start = ((bf16[4,2,6144]{2,1,0:T(2,128)(2,1)}), bf16[4,2,6144]{2,1,0:T(2,128)(2,1)S(1)}, u32[]{:S(2)}, u32[]{:S(2)}) async-start(bf16[4,2,6144]{2,1,0:T(2,128)(2,1)} %reshape.584), calls=%async_computation | async-start | bytes 196608 | tf_op jit(solution)/shard_map/all_to_all | solution.py:106
  49.1 4.1 %all-to-all-done = bf16[4,2,6144]{2,1,0:T(2,128)(2,1)S(1)} async-done(((bf16[4,2,6144]{2,1,0:T(2,128)(2,1)}), bf16[4,2,6144]{2,1,0:T(2,128)(2,1)S(1)}, u32[]{:S(2)}, u32[]{:S(2)}) %all-to-all-start) | async-done | bytes 98336 | tf_op jit(solution)/shard_map/all_to_all | solution.py:106
  53.2 4.8 %reshape.585 = bf16[4096,2,6]{2,1,0:T(2,128)(2,1)S(1)} reshape(bf16[4,2,6144]{2,1,0:T(2,128)(2,1)S(1)} %all-to-all-done) | data formatting | bytes 196608
  58.0 1.5 copy.141
  60.1 1.9 %collective-permute-start.1 = (bf16[2,128,1024]{2,1,0:T(8,128)(2,1)S(1)}, bf16[2,128,1024]{2,1,0:T(8,128)(2,1)S(1)}, u32[]{:S(2)}, u32[]{:S(2)}) collective-permute-start(bf16[2,128,1024]{2,1,0:T(8,128)(2,1)S(1)} %bitcast.233), channel_id=1, source_target_pairs={{0,4},{4,0},{8,12},{12,8},{16,20},{20,16},{24,28},{28,24},{32,36},... | collective-permute-start | bytes 1572872 | tf_op jit(solution)/shard_map/ppermute | solution.py:22
  62.9 13.0 %collective-permute-done.1 = bf16[2,128,1024]{2,1,0:T(8,128)(2,1)S(1)} collective-permute-done((bf16[2,128,1024]{2,1,0:T(8,128)(2,1)S(1)}, bf16[2,128,1024]{2,1,0:T(8,128)(2,1)S(1)}, u32[]{:S(2)}, u32[]{:S(2)}) %collective-permute-start.1) | collective-permute-done | bytes 524320 | tf_op jit(solution)/shard_map/ppermute | solution.py:22
  76.5 2.1 %collective-permute-start.2 = (bf16[2,128,1024]{2,1,0:T(8,128)(2,1)S(1)}, bf16[2,128,1024]{2,1,0:T(8,128)(2,1)S(1)}, u32[]{:S(2)}, u32[]{:S(2)}) collective-permute-start(bf16[2,128,1024]{2,1,0:T(8,128)(2,1)S(1)} %bitcast.247), channel_id=1, source_target_pairs={{0,8},{8,0},{4,12},{12,4},{16,24},{24,16},{20,28},{28,20},{32,40},... | collective-permute-start | bytes 1572872 | tf_op jit(solution)/shard_map/ppermute | solution.py:22
  79.4 24.4 %collective-permute-done.2 = bf16[2,128,1024]{2,1,0:T(8,128)(2,1)S(1)} collective-permute-done((bf16[2,128,1024]{2,1,0:T(8,128)(2,1)S(1)}, bf16[2,128,1024]{2,1,0:T(8,128)(2,1)S(1)}, u32[]{:S(2)}, u32[]{:S(2)}) %collective-permute-start.2) | collective-permute-done | bytes 524320 | tf_op jit(solution)/shard_map/ppermute | solution.py:22
  104.4 3.3 %collective-permute-start.3 = (bf16[2,128,1024]{2,1,0:T(8,128)(2,1)S(1)}, bf16[2,128,1024]{2,1,0:T(8,128)(2,1)S(1)}, u32[]{:S(2)}, u32[]{:S(2)}) collective-permute-start(bf16[2,128,1024]{2,1,0:T(8,128)(2,1)S(1)} %bitcast.248), channel_id=1, source_target_pairs={{0,16},{16,0},{4,20},{20,4},{8,24},{24,8},{12,28},{28,12},{32,48},... | collective-permute-start | bytes 1572872 | tf_op jit(solution)/shard_map/ppermute | solution.py:22
  108.6 24.8 %collective-permute-done.3 = bf16[2,128,1024]{2,1,0:T(8,128)(2,1)S(1)} collective-permute-done((bf16[2,128,1024]{2,1,0:T(8,128)(2,1)S(1)}, bf16[2,128,1024]{2,1,0:T(8,128)(2,1)S(1)}, u32[]{:S(2)}, u32[]{:S(2)}) %collective-permute-start.3) | collective-permute-done | bytes 524320 | tf_op jit(solution)/shard_map/ppermute | solution.py:22
  133.9 2.0 %collective-permute-start.4 = (bf16[2,128,1024]{2,1,0:T(8,128)(2,1)S(1)}, bf16[2,128,1024]{2,1,0:T(8,128)(2,1)S(1)}, u32[]{:S(2)}, u32[]{:S(2)}) collective-permute-start(bf16[2,128,1024]{2,1,0:T(8,128)(2,1)S(1)} %bitcast.249), channel_id=1, source_target_pairs={{0,32},{32,0},{4,36},{36,4},{8,40},{40,8},{12,44},{44,12},{16,48},... | collective-permute-start | bytes 1572872 | tf_op jit(solution)/shard_map/ppermute | solution.py:22
  136.6 12.7 %collective-permute-done.4 = bf16[2,128,1024]{2,1,0:T(8,128)(2,1)S(1)} collective-permute-done((bf16[2,128,1024]{2,1,0:T(8,128)(2,1)S(1)}, bf16[2,128,1024]{2,1,0:T(8,128)(2,1)S(1)}, u32[]{:S(2)}, u32[]{:S(2)}) %collective-permute-start.4) | collective-permute-done | bytes 524320 | tf_op jit(solution)/shard_map/ppermute | solution.py:22
  149.9 3.9 %collective-permute-start.5 = (bf16[2,128,1024]{2,1,0:T(8,128)(2,1)S(1)}, bf16[2,128,1024]{2,1,0:T(8,128)(2,1)S(1)}, u32[]{:S(2)}, u32[]{:S(2)}) collective-permute-start(bf16[2,128,1024]{2,1,0:T(8,128)(2,1)S(1)} %bitcast.250), channel_id=1, source_target_pairs={{0,64},{64,0},{4,68},{68,4},{8,72},{72,8},{12,76},{76,12},{16,80},... | collective-permute-start | bytes 1572872 | tf_op jit(solution)/shard_map/ppermute | solution.py:22
  153.9 22.7 %collective-permute-done.5 = bf16[2,128,1024]{2,1,0:T(8,128)(2,1)S(1)} collective-permute-done((bf16[2,128,1024]{2,1,0:T(8,128)(2,1)S(1)}, bf16[2,128,1024]{2,1,0:T(8,128)(2,1)S(1)}, u32[]{:S(2)}, u32[]{:S(2)}) %collective-permute-start.5) | collective-permute-done | bytes 524320 | tf_op jit(solution)/shard_map/ppermute | solution.py:22
  176.6 1.2 convolution_convert_fusion
  (160 shorter events, 12.3 us)
Async XLA Ops:
  0.0 19.2 %copy-start = (bf16[2,1,128,24]{2,3,1,0:T(8,128)(2,1)S(1)}, bf16[2,1,128,24]{2,3,1,0:T(8,128)(2,1)}, u32[]{:S(2)}) copy-start(bf16[2,1,128,24]{2,3,1,0:T(8,128)(2,1)} %param.11) | copy-start | bytes 36868
  1.5 27.8 %collective-permute-start = (bf16[2,6,2048]{2,0,1:T(2,128)(2,1)}, bf16[2,6,2048]{2,0,1:T(2,128)(2,1)}, u32[]{:S(2)}, u32[]{:S(2)}) collective-permute-start(bf16[2,6,2048]{2,0,1:T(2,128)(2,1)} %slice.437), channel_id=1, source_target_pairs={{1,0},{2,1},{3,2},{5,4},{6,5},{7,6},{9,8},{10,9},{11,10},{13,12},{... | collective-permute-start | bytes 147464 | tf_op jit(solution)/shard_map/ppermute | solution.py:12
  12.9 1.1 copy-start.27
  12.9 1.6 copy-start.28
  12.9 2.1 %copy-start.4 = (bf16[5,1,2,2,128,16]{4,5,3,2,1,0:T(8,128)(2,1)S(1)}, bf16[5,1,2,2,128,16]{4,5,3,2,1,0:T(8,128)(2,1)}, u32[]{:S(2)}) copy-start(bf16[5,1,2,2,128,16]{4,5,3,2,1,0:T(8,128)(2,1)} %param.13) | copy-start | bytes 245764
  14.0 5.2 %copy-start.34 = (s32[1,24]{1,0:T(1,128)S(1)}, s32[1,24]{1,0:T(1,128)}, u32[]{:S(2)}) copy-start(s32[1,24]{1,0:T(1,128)} %param.12) | copy-start | bytes 292
  19.4 4.2 %copy-start.23 = (bf16[2,128,24]{1,2,0:T(8,128)(2,1)}, bf16[2,128,24]{1,2,0:T(8,128)(2,1)S(1)}, u32[]{:S(2)}) copy-start(bf16[2,128,24]{1,2,0:T(8,128)(2,1)S(1)} %fusion.14) | copy-start | bytes 36868
  34.4 14.7 %copy-start.24 = (bf16[2,128,24]{1,2,0:T(8,128)(2,1)S(1)}, bf16[2,128,24]{1,2,0:T(8,128)(2,1)}, u32[]{:S(2)}) copy-start(bf16[2,128,24]{1,2,0:T(8,128)(2,1)} %copy-done.23) | copy-start | bytes 36868
  40.0 13.2 %all-to-all-start = ((bf16[4,2,6144]{2,1,0:T(2,128)(2,1)}), bf16[4,2,6144]{2,1,0:T(2,128)(2,1)S(1)}, u32[]{:S(2)}, u32[]{:S(2)}) async-start(bf16[4,2,6144]{2,1,0:T(2,128)(2,1)} %reshape.584), calls=%async_computation | async-start | bytes 196608 | tf_op jit(solution)/shard_map/all_to_all | solution.py:106
  49.1 10.6 %copy-start.25 = (bf16[128,24]{0,1:T(8,128)(2,1)S(1)}, bf16[128,24]{0,1:T(8,128)(2,1)}, u32[]{:S(2)}) copy-start(bf16[128,24]{0,1:T(8,128)(2,1)} %get-tuple-element.172) | copy-start | bytes 18436
  49.1 10.6 %copy-start.26 = (bf16[128,24]{0,1:T(8,128)(2,1)S(1)}, bf16[128,24]{0,1:T(8,128)(2,1)}, u32[]{:S(2)}) copy-start(bf16[128,24]{0,1:T(8,128)(2,1)} %get-tuple-element.173) | copy-start | bytes 18436
  57.9 4.0 %copy-start.32 = (s32[128]{0:T(128)S(1)}, s32[128]{0:T(128)}, u32[]{:S(2)}) copy-start(s32[128]{0:T(128)} %get-tuple-element.179) | copy-start | bytes 1540
  58.0 4.0 %copy-start.33 = (s32[128]{0:T(128)S(1)}, s32[128]{0:T(128)}, u32[]{:S(2)}) copy-start(s32[128]{0:T(128)} %get-tuple-element.180) | copy-start | bytes 1540
  58.0 4.2 %copy-start.2 = (bf16[1,128,128]{2,0,1:T(2,128)(2,1)S(1)}, bf16[1,128,128]{2,0,1:T(2,128)(2,1)}, u32[]{:S(2)}) copy-start(bf16[1,128,128]{2,0,1:T(2,128)(2,1)} %get-tuple-element.171) | copy-start | bytes 98308
  58.0 4.2 %copy-start.10 = (bf16[1,1,1,2,128,16]{4,5,3,2,1,0:T(8,128)(2,1)S(1)}, bf16[1,1,1,2,128,16]{4,5,3,2,1,0:T(8,128)(2,1)}, u32[]{:S(2)}) copy-start(bf16[1,1,1,2,128,16]{4,5,3,2,1,0:T(8,128)(2,1)} %get-tuple-element.149) | copy-start | bytes 24580
  58.0 4.3 %copy-start.6 = (s32[128,128]{1,0:T(8,128)S(1)}, s32[128,128]{1,0:T(8,128)}, u32[]{:S(2)}) copy-start(s32[128,128]{1,0:T(8,128)} %get-tuple-element.201) | copy-start | bytes 196612
  59.5 16.4 %copy-start.15 = (bf16[128,128]{1,0:T(8,128)(2,1)S(1)}, bf16[128,128]{1,0:T(8,128)(2,1)}, u32[]{:S(2)}) copy-start(bf16[128,128]{1,0:T(8,128)(2,1)} %get-tuple-element.124) | copy-start | bytes 98308
  59.5 16.4 %copy-start.16 = (bf16[128,128]{1,0:T(8,128)(2,1)S(1)}, bf16[128,128]{1,0:T(8,128)(2,1)}, u32[]{:S(2)}) copy-start(bf16[128,128]{1,0:T(8,128)(2,1)} %get-tuple-element.125) | copy-start | bytes 98308
  59.5 16.4 %copy-start.21 = (bf16[128,128]{1,0:T(8,128)(2,1)S(1)}, bf16[128,128]{1,0:T(8,128)(2,1)}, u32[]{:S(2)}) copy-start(bf16[128,128]{1,0:T(8,128)(2,1)} %get-tuple-element.126) | copy-start | bytes 98308
  59.5 16.4 %copy-start.22 = (bf16[128,128]{1,0:T(8,128)(2,1)S(1)}, bf16[128,128]{1,0:T(8,128)(2,1)}, u32[]{:S(2)}) copy-start(bf16[128,128]{1,0:T(8,128)(2,1)} %get-tuple-element.127) | copy-start | bytes 98308
  60.1 15.8 %collective-permute-start.1 = (bf16[2,128,1024]{2,1,0:T(8,128)(2,1)S(1)}, bf16[2,128,1024]{2,1,0:T(8,128)(2,1)S(1)}, u32[]{:S(2)}, u32[]{:S(2)}) collective-permute-start(bf16[2,128,1024]{2,1,0:T(8,128)(2,1)S(1)} %bitcast.233), channel_id=1, source_target_pairs={{0,4},{4,0},{8,12},{12,8},{16,20},{20,16},{24,28},{28,24},{32,36},... | collective-permute-start | bytes 1572872 | tf_op jit(solution)/shard_map/ppermute | solution.py:22
  76.0 2.6 %copy-start.3 = (bf16[1,128,128]{2,0,1:T(2,128)(2,1)S(1)}, bf16[1,128,128]{2,0,1:T(2,128)(2,1)}, u32[]{:S(2)}) copy-start(bf16[1,128,128]{2,0,1:T(2,128)(2,1)} %get-tuple-element.167) | copy-start | bytes 98308
  76.0 2.7 %copy-start.9 = (bf16[1,1,1,2,128,16]{4,5,3,2,1,0:T(8,128)(2,1)S(1)}, bf16[1,1,1,2,128,16]{4,5,3,2,1,0:T(8,128)(2,1)}, u32[]{:S(2)}) copy-start(bf16[1,1,1,2,128,16]{4,5,3,2,1,0:T(8,128)(2,1)} %get-tuple-element.148) | copy-start | bytes 24580
  76.0 2.8 %copy-start.30 = (s32[128]{0:T(128)S(1)}, s32[128]{0:T(128)}, u32[]{:S(2)}) copy-start(s32[128]{0:T(128)} %get-tuple-element.184) | copy-start | bytes 1540
  76.0 2.8 %copy-start.31 = (s32[128]{0:T(128)S(1)}, s32[128]{0:T(128)}, u32[]{:S(2)}) copy-start(s32[128]{0:T(128)} %get-tuple-element.191) | copy-start | bytes 1540
  76.0 2.9 %copy-start.5 = (s32[128,128]{1,0:T(8,128)S(1)}, s32[128,128]{1,0:T(8,128)}, u32[]{:S(2)}) copy-start(s32[128,128]{1,0:T(8,128)} %get-tuple-element.200) | copy-start | bytes 196612
  76.5 27.4 %copy-start.13 = (bf16[128,128]{1,0:T(8,128)(2,1)S(1)}, bf16[128,128]{1,0:T(8,128)(2,1)}, u32[]{:S(2)}) copy-start(bf16[128,128]{1,0:T(8,128)(2,1)} %get-tuple-element.120) | copy-start | bytes 98308
  76.5 27.4 %copy-start.14 = (bf16[128,128]{1,0:T(8,128)(2,1)S(1)}, bf16[128,128]{1,0:T(8,128)(2,1)}, u32[]{:S(2)}) copy-start(bf16[128,128]{1,0:T(8,128)(2,1)} %get-tuple-element.121) | copy-start | bytes 98308
  76.5 27.4 %copy-start.19 = (bf16[128,128]{1,0:T(8,128)(2,1)S(1)}, bf16[128,128]{1,0:T(8,128)(2,1)}, u32[]{:S(2)}) copy-start(bf16[128,128]{1,0:T(8,128)(2,1)} %get-tuple-element.122) | copy-start | bytes 98308
  76.5 27.4 %copy-start.20 = (bf16[128,128]{1,0:T(8,128)(2,1)S(1)}, bf16[128,128]{1,0:T(8,128)(2,1)}, u32[]{:S(2)}) copy-start(bf16[128,128]{1,0:T(8,128)(2,1)} %get-tuple-element.123) | copy-start | bytes 98308
  76.5 27.3 %collective-permute-start.2 = (bf16[2,128,1024]{2,1,0:T(8,128)(2,1)S(1)}, bf16[2,128,1024]{2,1,0:T(8,128)(2,1)S(1)}, u32[]{:S(2)}, u32[]{:S(2)}) collective-permute-start(bf16[2,128,1024]{2,1,0:T(8,128)(2,1)S(1)} %bitcast.247), channel_id=1, source_target_pairs={{0,8},{8,0},{4,12},{12,4},{16,24},{24,16},{20,28},{28,20},{32,40},... | collective-permute-start | bytes 1572872 | tf_op jit(solution)/shard_map/ppermute | solution.py:22
  103.9 3.8 %copy-start.29 = (s32[128]{0:T(128)S(1)}, s32[128]{0:T(128)}, u32[]{:S(2)}) copy-start(s32[128]{0:T(128)} %get-tuple-element.181) | copy-start | bytes 1540
  103.9 3.9 %copy-start.1 = (bf16[1,128,128]{2,0,1:T(2,128)(2,1)S(1)}, bf16[1,128,128]{2,0,1:T(2,128)(2,1)}, u32[]{:S(2)}) copy-start(bf16[1,128,128]{2,0,1:T(2,128)(2,1)} %get-tuple-element.163) | copy-start | bytes 98308
  103.9 4.0 %copy-start.8 = (bf16[1,1,1,2,128,16]{4,5,3,2,1,0:T(8,128)(2,1)S(1)}, bf16[1,1,1,2,128,16]{4,5,3,2,1,0:T(8,128)(2,1)}, u32[]{:S(2)}) copy-start(bf16[1,1,1,2,128,16]{4,5,3,2,1,0:T(8,128)(2,1)} %get-tuple-element.142) | copy-start | bytes 24580
  104.3 29.0 %copy-start.11 = (bf16[128,128]{1,0:T(8,128)(2,1)S(1)}, bf16[128,128]{1,0:T(8,128)(2,1)}, u32[]{:S(2)}) copy-start(bf16[128,128]{1,0:T(8,128)(2,1)} %get-tuple-element.116) | copy-start | bytes 98308
  104.4 29.0 %copy-start.12 = (bf16[128,128]{1,0:T(8,128)(2,1)S(1)}, bf16[128,128]{1,0:T(8,128)(2,1)}, u32[]{:S(2)}) copy-start(bf16[128,128]{1,0:T(8,128)(2,1)} %get-tuple-element.117) | copy-start | bytes 98308
  104.4 29.0 %copy-start.17 = (bf16[128,128]{1,0:T(8,128)(2,1)S(1)}, bf16[128,128]{1,0:T(8,128)(2,1)}, u32[]{:S(2)}) copy-start(bf16[128,128]{1,0:T(8,128)(2,1)} %get-tuple-element.118) | copy-start | bytes 98308
  104.4 29.0 %copy-start.18 = (bf16[128,128]{1,0:T(8,128)(2,1)S(1)}, bf16[128,128]{1,0:T(8,128)(2,1)}, u32[]{:S(2)}) copy-start(bf16[128,128]{1,0:T(8,128)(2,1)} %get-tuple-element.119) | copy-start | bytes 98308
  104.4 28.9 %collective-permute-start.3 = (bf16[2,128,1024]{2,1,0:T(8,128)(2,1)S(1)}, bf16[2,128,1024]{2,1,0:T(8,128)(2,1)S(1)}, u32[]{:S(2)}, u32[]{:S(2)}) collective-permute-start(bf16[2,128,1024]{2,1,0:T(8,128)(2,1)S(1)} %bitcast.248), channel_id=1, source_target_pairs={{0,16},{16,0},{4,20},{20,4},{8,24},{24,8},{12,28},{28,12},{32,48},... | collective-permute-start | bytes 1572872 | tf_op jit(solution)/shard_map/ppermute | solution.py:22
  133.4 2.5 %copy-start.7 = (bf16[1,1,1,2,128,16]{4,5,3,2,1,0:T(8,128)(2,1)S(1)}, bf16[1,1,1,2,128,16]{4,5,3,2,1,0:T(8,128)(2,1)}, u32[]{:S(2)}) copy-start(bf16[1,1,1,2,128,16]{4,5,3,2,1,0:T(8,128)(2,1)} %get-tuple-element.150) | copy-start | bytes 24580
  133.9 15.5 %collective-permute-start.4 = (bf16[2,128,1024]{2,1,0:T(8,128)(2,1)S(1)}, bf16[2,128,1024]{2,1,0:T(8,128)(2,1)S(1)}, u32[]{:S(2)}, u32[]{:S(2)}) collective-permute-start(bf16[2,128,1024]{2,1,0:T(8,128)(2,1)S(1)} %bitcast.249), channel_id=1, source_target_pairs={{0,32},{32,0},{4,36},{36,4},{8,40},{40,8},{12,44},{44,12},{16,48},... | collective-permute-start | bytes 1572872 | tf_op jit(solution)/shard_map/ppermute | solution.py:22
  149.9 26.7 %collective-permute-start.5 = (bf16[2,128,1024]{2,1,0:T(8,128)(2,1)S(1)}, bf16[2,128,1024]{2,1,0:T(8,128)(2,1)S(1)}, u32[]{:S(2)}, u32[]{:S(2)}) collective-permute-start(bf16[2,128,1024]{2,1,0:T(8,128)(2,1)S(1)} %bitcast.250), channel_id=1, source_target_pairs={{0,64},{64,0},{4,68},{68,4},{8,72},{72,8},{12,76},{76,12},{16,80},... | collective-permute-start | bytes 1572872 | tf_op jit(solution)/shard_map/ppermute | solution.py:22
where the time goes:
time: 181 us; the launch traced here: 178 us
  waiting for transfers between devices  102 us (56%)
  local copies, waits for them, and re-layouts  29.8 us (16%)
  starting transfers between devices  23.6 us (13%)
  matrix products  11.7 us (6%)
  other arithmetic  9.67 us (5%)
    ppermute x5, waiting for transfers between devices, from_partner(): return lax.ppermute(block, axis, route)  97.6 us
    unnamed x95, local copies, waits for them, and re-layouts  13.9 us
    ppermute x5, starting transfers between devices, from_partner(): return lax.ppermute(block, axis, route)  13.1 us
    all_to_all x1, starting transfers between devices, on_device(): lax.all_to_all(compressed, 'section', split_axis=2, concat_axis=1, tiled=...  9.13 us
    dot_general x10, matrix products, band_matrix(): jnp.einsum('sqt,tqc->sqc', coef_side, selector, preferred_element_type=jn...  4.58 us
    all_to_all x1, waiting for transfers between devices, on_device(): lax.all_to_all(compressed, 'section', split_axis=2, concat_axis=1, tiled=...  4.06 us
  transfers between devices with their start and end apart: 7, of which 6 were waited for; matrix products, arithmetic and copies ran while one was open for 17% of the time, Pallas kernels for 0%

commit v1 on v0

v1 whole, which is shorter than its diff:
```python
import functools

import jax
import jax.numpy as jnp
from jax import lax
from jax.experimental import pallas as pl
from jax.experimental.pallas import tpu as pltpu
from jax.sharding import PartitionSpec as P

F32 = jnp.float32
BF16 = jnp.bfloat16
MESH = pl.DeviceIdType.MESH

NX = 4
NY = 8
NZ = 4
NG = 4
PP = 6
PS = 24
RC = 4096
TAPS = 2048
CB = 128
QB = 128
SEC = 1024
NCH = 4
CW = SEC // NCH
BLK = 4 * PS
GROUPS = ((0, 1), (2, 3))


def dot(a, b):
    return jnp.dot(a, b, preferred_element_type=F32)


def dot_nt(a, b):
    return lax.dot_general(a, b, (((1,), (1,)), ((), ())), preferred_element_type=F32)


def flip(v, bit):
    return v + bit - 2 * bit * ((v // bit) % 2)


def one_hot(shape, dim0_of_dim1):
    rows = lax.broadcasted_iota(jnp.int32, shape, 0)
    cols = lax.broadcasted_iota(jnp.int32, shape, 1)
    return jnp.where(rows == dim0_of_dim1(cols), 1.0, 0.0).astype(BF16)


def kernel(
    echo, chirp, steer, order, coef, start, width, out,
    halo, xf, x2, table, comp, recv, gath, pmat, zcoef, zstart, mats,
    tx0, tx1, tx2, tx3, ts, tt, tmat, own, psend, precv, ostage,
    s_rim, r_rim, s_par, r_par, s_t, r_t, s_a, r_a, s_g, r_g, s_p, r_p, s_o,
):
    sec = lax.axis_index("section")
    sub = lax.axis_index("sub")
    rng = lax.axis_index("rng")
    y = sub % NY
    z = sub // NY
    base = z * NY

    def at_y(v):
        return {"sub": base + v}

    def at_z(v):
        return {"sub": v * NY + y}

    z1 = flip(z, 1)
    z2 = flip(z, 2)
    z3 = flip(z2, 1)
    y1 = flip(y, 1)
    y2 = flip(y, 2)
    y4 = flip(y, 4)
    up = (y + 1) % NY
    down = (y + NY - 1) % NY

    barrier = pltpu.get_barrier_semaphore()
    peers = [{"rng": (rng + 1) % NG}, {"rng": (rng + NG - 1) % NG}]
    for d in range(1, NX):
        other = (sec + d) % NX
        peers.append({"section": other})
        peers.append({"section": other, "sub": z2 * NY + y})
    peers += [at_z(z1), at_z(z2), at_z(z3), at_y(up), at_y(down), at_y(flip(y, 2)), at_y(y4)]
    for peer in peers:
        pl.semaphore_signal(barrier, inc=1, device_id=peer, device_id_type=MESH)
    pl.semaphore_wait(barrier, len(peers))

    def send(src, dst, ssem, rsem, to):
        return pltpu.make_async_remote_copy(
            src_ref=src, dst_ref=dst, send_sem=ssem, recv_sem=rsem,
            device_id=to, device_id_type=MESH,
        )

    rim = send(echo.at[:, :, 0:TAPS], halo, s_rim, r_rim, {"rng": (rng + NG - 1) % NG})
    rim.start()

    select = one_hot((PS, PS), lambda cols: order[...])
    eye32 = one_hot((32, PS), lambda cols: cols)
    sel_t = dot_nt(eye32, select).astype(BF16)
    ts[0:32, 0:QB] = dot(sel_t, steer[0]).astype(BF16)
    ts[0:32, QB:] = dot(sel_t, steer[1]).astype(BF16)
    t0 = send(ts.at[0:32], tx0, s_t.at[0], r_t.at[0], at_y(y1))
    t0.start()

    taps = lax.broadcasted_iota(jnp.int32, (16, QB), 0)
    for level in range(5):
        for side in range(2):
            keep = taps < width[level, side : side + 1, :]
            for part in range(2):
                i = level * 4 + side * 2 + part
                entry = jnp.where(keep, coef[i].astype(F32), 0.0)
                pmat[i] = entry.astype(BF16)
                if level >= 3:
                    zcoef[0, i - 12] = entry.astype(BF16)
            if level >= 3:
                zstart[0, (level - 3) * 2 + side : (level - 3) * 2 + side + 1, :] = start[level, side : side + 1, :]
    zstart[0, 4:8, :] = jnp.zeros((4, QB), jnp.int32)
    par = []
    for d, to in ((1, z1), (2, z2), (3, z3)):
        par.append(send(zcoef.at[0], zcoef.at[d], s_par.at[0, d], r_par.at[0, d], at_z(to)))
        par.append(send(zstart.at[0], zstart.at[d], s_par.at[1, d], r_par.at[1, d], at_z(to)))
    for copy in par:
        copy.start()

    def band(slot, real, imag, first):
        offset = lax.broadcasted_iota(jnp.int32, (QB, QB), 0) - first
        re = jnp.zeros((QB, QB), F32)
        im = jnp.zeros((QB, QB), F32)
        for t in range(16):
            hit = offset == t
            re = jnp.where(hit, real[t : t + 1, :], re)
            im = jnp.where(hit, imag[t : t + 1, :], im)
        re_b = re.astype(BF16)
        mats[slot, 0:QB, 0:QB] = re_b
        mats[slot, QB:, QB:] = re_b
        mats[slot, 0:QB, QB:] = im.astype(BF16)
        mats[slot, QB:, 0:QB] = (-im).astype(BF16)

    def own_band(level, side):
        i = level * 4 + side * 2
        band(level * 2 + side, pmat[i].astype(F32), pmat[i + 1].astype(F32), start[level, side : side + 1, :])

    def far_band(slot, d, row):
        band(slot, zcoef[d, row * 2].astype(F32), zcoef[d, row * 2 + 1].astype(F32), zstart[d, row : row + 1, :])

    wide = TAPS + 2 * CB
    for part in range(2):
        line = jnp.concatenate([chirp[part : part + 1, :].astype(F32), jnp.zeros((1, 2 * CB), F32)], axis=1)
        line = jnp.broadcast_to(line, (CB, wide))
        table[part * CB : (part + 1) * CB, :] = pltpu.roll(line, 0, 1, stride=1, stride_axis=0).astype(BF16)

    def load_rows(ref, blocks, first):
        lanes = blocks * CB
        for part in range(2):
            for p in range(PP):
                xf[part * 8 + p : part * 8 + p + 1, 0:lanes] = ref[p, part : part + 1, :].astype(F32)
            xf[part * 8 + PP : part * 8 + 8, 0:lanes] = jnp.zeros((8 - PP, lanes), F32)
        for b in range(blocks):
            tile = xf[:, b * CB : (b + 1) * CB]
            if ref is halo:
                tile = jnp.where(rng == NG - 1, jnp.zeros_like(tile), tile)
            tile = tile.astype(BF16)
            x2[first + b, :, 0:CB] = tile
            if first + b > 0:
                x2[first + b - 1, :, CB:] = tile

    nb = RC // CB
    nh = TAPS // CB

    def compress(first):
        rows = 16
        total = None
        for j in range(wide // (2 * CB)):
            lhs = x2[first + 2 * j : first + 2 * j + rows].reshape(rows * 16, 2 * CB)
            piece = dot_nt(lhs, table[:, 2 * j * CB : 2 * (j + 1) * CB])
            total = piece if total is None else total + piece
        for b in range(rows):
            re_rows = total[b * 16 : b * 16 + 8]
            im_rows = total[b * 16 + 8 : b * 16 + 16]
            re = re_rows[:, 0:CB] + im_rows[:, CB:]
            im = im_rows[:, 0:CB] - re_rows[:, CB:]
            at = (first + b) * CB
            comp[:, at : at + CB] = jnp.concatenate([re, im], axis=0).astype(BF16)

    def scatter(s):
        lanes = comp.at[:, s * SEC : (s + 1) * SEC]
        near = send(lanes, recv.at[0, sec], s_a.at[0, s], r_a.at[0, sec], {"section": s})
        far = send(lanes, recv.at[1, sec], s_a.at[1, s], r_a.at[1, sec], {"section": s, "sub": z2 * NY + y})
        far.start()

        @pl.when(sec != s)
        def _():
            near.start()

        return near, far

    load_rows(echo, nb, 0)
    compress(0)
    sent = [scatter(0), scatter(1)]
    rim.wait()
    load_rows(halo, nh, nb)
    x2[nb + nh - 1, :, CB:] = jnp.zeros((16, CB), BF16)
    compress(16)
    sent += [scatter(2), scatter(3)]
    recv[0, sec] = comp[:, pl.ds(pl.multiple_of(sec * SEC, SEC), SEC)]

    def grow(level, mine, theirs, rows):
        at_low = (y // (1 << level)) % 2 == 0
        a = dot(mine, mats[level * 2])[0:rows]
        b = dot(theirs, mats[level * 2 + 1])[0:rows]
        low = jnp.where(at_low, a, b)
        high = jnp.where(at_low, b, a)
        return jnp.concatenate([low, high], axis=0).astype(BF16)

    own_band(0, 0)
    own_band(0, 1)
    t0.wait()
    ts[32:80] = grow(0, ts[0:32], tx0[...], PS)
    t1 = send(ts.at[32:80], tx1, s_t.at[1], r_t.at[1], at_y(y2))
    t1.start()

    for x in range(NX):
        for zz in range(2):
            arrival = send(comp.at[:, 0:SEC], recv.at[zz, x], s_a.at[zz, 0], r_a.at[zz, x], {"section": sec})
            if zz == 0:
                @pl.when(sec != x)
                def _():
                    arrival.wait_recv()
            else:
                arrival.wait_recv()
    rows_i = lax.broadcasted_iota(jnp.int32, (BLK, 128), 0)
    cols_i = lax.broadcasted_iota(jnp.int32, (BLK, 128), 1)
    hot = jnp.zeros((BLK, 128), F32)
    for zz in range(2):
        for part in range(2):
            for x in range(NX):
                r0 = zz * 2 * PS + part * PS + x * PP
                c0 = zz * 64 + x * 16 + part * 8
                inside = (rows_i >= r0) & (rows_i < r0 + PP) & (cols_i - rows_i == c0 - r0)
                hot = jnp.where(inside, 1.0, hot)
    hot = hot.astype(BF16)
    for c in range(NCH):
        rows = recv[:, :, :, c * CW : (c + 1) * CW].reshape(2 * NX * 16, CW)
        gath[c, y] = dot(hot, rows).astype(BF16)

    def hop(direction, c, s):
        if direction == 0:
            at = (y + NY - s) % NY
            to = up
        else:
            at = (y + s) % NY
            to = down
        return send(gath.at[c, at], gath.at[c, at], s_g.at[direction, c, s], r_g.at[direction, c, s], at_y(to))

    def arrived(direction, c, s):
        if direction == 0:
            at = (y + 2 * NY - 1 - s) % NY
        else:
            at = (y + 1 + s) % NY
        return send(gath.at[c, at], gath.at[c, at], s_g.at[direction, c, s], r_g.at[direction, c, s], at_y(up))

    def legs(c, s):
        return (0, 1) if s < 3 else (c % 2,)

    def ring(group, s):
        for c in GROUPS[group]:
            for direction in legs(c, s):
                if s > 0:
                    arrived(direction, c, s - 1).wait_recv()
                hop(direction, c, s).start()

    def settle(group):
        for c in GROUPS[group]:
            for direction in (0, 1):
                last = 3 if direction in legs(c, 3) else 2
                if last == 3:
                    arrived(direction, c, 3).wait_recv()
                else:
                    arrived(direction, c, 2).wait_recv()

    ring(0, 0)
    ring(1, 0)
    own_band(1, 0)
    own_band(1, 1)
    t1.wait()
    ts[80:176] = grow(1, ts[32:80], tx1[...], 2 * PS)
    t2 = send(ts.at[80:176], tx2, s_t.at[2], r_t.at[2], at_y(y4))
    t2.start()
    ring(0, 1)
    own_band(2, 0)
    own_band(2, 1)
    ring(1, 1)
    t2.wait()
    ts[176:368] = grow(2, ts[80:176], tx2[...], 4 * PS)
    t3 = send(ts.at[176:368], tx3, s_t.at[3], r_t.at[3], at_z(z2))
    t3.start()
    ring(0, 2)
    for level in (3, 4):
        for side in range(2):
            own_band(level, side)
    for copy in par:
        copy.wait()
    far_band(10, 1, 1)
    far_band(11, 1, 2)
    far_band(12, 1, 3)
    ring(1, 2)
    far_band(13, 2, 0)
    far_band(14, 3, 1)
    ring(0, 3)

    def chain(rows, first, second):
        return dot(dot(rows, mats[first]).astype(BF16), mats[second]).reshape(NY, PS, 2 * QB)

    def turned(rows):
        return jnp.concatenate([-rows[:, :, QB:], rows[:, :, 0:QB]], axis=2)

    eye = one_hot((2 * QB, 2 * QB), lambda cols: cols)
    near_rows = ts[176:368]
    a0 = chain(near_rows, 6, 8)
    b0 = chain(near_rows, 10, 11)
    t3.wait()
    far_rows = tx3[...]
    a1 = chain(far_rows, 13, 9)
    b1 = chain(far_rows, 14, 12)
    for i, (near_t, far_t) in enumerate(((a0, a1), (b0, b1))):
        full = jnp.concatenate([near_t, turned(near_t), far_t, turned(far_t)], axis=1)
        tt[...] = full.reshape(NY * BLK, 2 * QB).astype(BF16)
        tmat[i * 2 * QB : (i + 1) * 2 * QB, :] = dot_nt(eye, tt[...]).astype(BF16)
    ring(1, 3)

    swaps = []
    for group in range(2):
        settle(group)
        for c in GROUPS[group]:
            pulses = gath[c].reshape(NY * BLK, CW)
            psend[c] = dot(tmat[2 * QB :, :], pulses).astype(BF16)
            swap = send(psend.at[c], precv.at[c], s_p.at[c], r_p.at[c], at_z(z1))
            swap.start()
            swaps.append(swap)
            own[c] = dot(tmat[0 : 2 * QB, :], pulses)
    stores = []
    for c in range(NCH):
        swaps[c].wait()
        total = own[c] + precv[c].astype(F32)
        ostage[c] = total.reshape(2, QB, CW).astype(BF16)
        store = pltpu.make_async_copy(ostage.at[c], out.at[:, :, c * CW : (c + 1) * CW], s_o.at[c])
        store.start()
        stores.append(store)
    for store in stores:
        store.wait()
    for s, (near, far) in enumerate(sent):
        far.wait_send()

        @pl.when(sec != s)
        def _():
            near.wait_send()

    for c in range(NCH):
        for s in range(4):
            for direction in legs(c, s):
                hop(direction, c, s).wait_send()


def on_device(echoes, chirp, steer, pulse_order, band_coef, band_start, band_width):
    echo = jnp.transpose(echoes[:, 0], (1, 0, 2))
    steer_t = jnp.swapaxes(steer[:, 0], 1, 2)
    coef = jnp.swapaxes(band_coef[:, 0], 3, 4).reshape(20, 16, QB)
    dma = pltpu.SemaphoreType.DMA
    vmem = pltpu.VMEM
    image = pl.pallas_call(
        kernel,
        out_shape=jax.ShapeDtypeStruct((2, QB, SEC), BF16),
        in_specs=[pl.BlockSpec(memory_space=pltpu.VMEM)] * 7,
        out_specs=pl.BlockSpec(memory_space=pl.ANY),
        scratch_shapes=[
            vmem((PP, 2, TAPS), BF16),
            vmem((16, RC), F32),
            vmem((48, 16, 2 * CB), BF16),
            vmem((2 * CB, TAPS + 2 * CB), BF16),
            vmem((16, RC), BF16),
            vmem((2, NX, 16, SEC), BF16),
            vmem((NCH, NY, BLK, CW), BF16),
            vmem((20, 16, QB), BF16),
            vmem((4, 8, 16, QB), BF16),
            vmem((4, 8, QB), jnp.int32),
            vmem((15, 2 * QB, 2 * QB), BF16),
            vmem((32, 2 * QB), BF16),
            vmem((2 * PS, 2 * QB), BF16),
            vmem((4 * PS, 2 * QB), BF16),
            vmem((8 * PS, 2 * QB), BF16),
            vmem((368, 2 * QB), BF16),
            vmem((NY * BLK, 2 * QB), BF16),
            vmem((4 * QB, NY * BLK), BF16),
            vmem((NCH, 2 * QB, CW), F32),
            vmem((NCH, 2 * QB, CW), BF16),
            vmem((NCH, 2 * QB, CW), BF16),
            vmem((NCH, 2, QB, CW), BF16),
            dma, dma,
            dma((2, 4)), dma((2, 4)),
            dma((4,)), dma((4,)),
            dma((2, NX)), dma((2, NX)),
            dma((2, NCH, 4)), dma((2, NCH, 4)),
            dma((NCH,)), dma((NCH,)),
            dma((NCH,)),
        ],
        compiler_params=pltpu.CompilerParams(
            collective_id=0, has_side_effects=True, vmem_limit_bytes=40 << 20
        ),
        name="aperture",
    )(echo, chirp, steer_t, pulse_order, coef, band_start[:, 0], band_width[:, 0])
    return image[:, :, None, :]


def solution(mesh):
    return jax.shard_map(
        on_device,
        mesh=mesh,
        in_specs=(
            P(None, "sub", "section", "rng"),
            P(),
            P(None, "sub", None, None),
            P("sub", None),
            P(None, "sub", None, None, None, None),
            P(None, "sub", None, None),
            P(None, "sub", None, None),
        ),
        out_specs=P(None, "sub", "rng", "section"),
        check_vma=False,
    )
```

time: 181 us -> 63.1 us (0.35); the launches traced: 178 us -> 62.7 us
  waiting for transfers between devices: 102 us -> 0 us
  Pallas kernels: 0 us -> 57.3 us
  local copies, waits for them, and re-layouts: 29.8 us -> 5.36 us
  starting transfers between devices: 23.6 us -> 0 us
  matrix products: 11.7 us -> 0 us
  other arithmetic: 9.67 us -> 0 us
    ppermute x6 -> x0, waiting for transfers between devices: 97.6 us -> none  [the longest x5 97.6 us: from_partner(): return lax.ppermute(block, axis, route)]
    pallas_call x0 -> x1, Pallas kernels: none -> 57.3 us  [on_device(): pl.pallas_call(kernel, out_shape=jax.ShapeDtypeStruct((2, QB, SEC), BF16)...]
    ppermute x6 -> x0, starting transfers between devices: 14.4 us -> none  [the longest x5 13.1 us: from_partner(): return lax.ppermute(block, axis, route)]
    dot_general x34 -> x0, matrix products: 11.7 us -> none  [the longest x10 4.58 us: band_matrix(): jnp.einsum('sqt,tqc->sqc', coef_side, selector, preferred_element_type=jn...]
    all_to_all x1 -> x0, starting transfers between devices: 9.13 us -> none  [on_device(): lax.all_to_all(compressed, 'section', split_axis=2, concat_axis=1, tiled=...]
    slice x18 -> x0, local copies, waits for them, and re-layouts: 8.69 us -> none  [the longest x2 2.75 us: lag_tables(): tiled.reshape(2, CBLK, total_len - 1)]
    unnamed x95 -> x15, local copies, waits for them, and re-layouts: 13.9 us -> 5.36 us
    neg x12 -> x0, other arithmetic: 4.78 us -> none  [the longest x5 1.95 us: merge_level(): -self_matrix[1]]
  transfers between devices with their start and end apart: 7 -> 0, of which waited for: 6 -> 0; matrix products, arithmetic and copies ran while one was open for 17% -> 0% of each run, Pallas kernels for 0% -> 0%
where the time goes in v1:
time: 63.1 us; the launch traced here: 62.7 us
  Pallas kernels  57.3 us (91%)
  local copies, waits for them, and re-layouts  5.36 us (8%)
    pallas_call x1, Pallas kernels, on_device(): pl.pallas_call(kernel, out_shape=jax.ShapeDtypeStruct((2, QB, SEC), BF16)...  57.3 us
    unnamed x15, local copies, waits for them, and re-layouts  5.36 us

profile of v1, /device:TPU:6, one launch (start us, length us, event | category | flops | bytes accessed | tf_op | source)
XLA Modules:
  0.0 62.7 jit_solution(13642388544041222425)
XLA Ops:
  0.0 0.0 copy-start.3
  0.0 0.0 copy-start.6
  0.0 0.7 %copy-done.3 = bf16[2,2048]{1,0:T(2,128)(2,1)S(1)} copy-done((bf16[2,2048]{1,0:T(2,128)(2,1)S(1)}, bf16[2,2048]{1,0:T(2,128)(2,1)}, u32[]{:S(2)}) %copy-start.3) | copy-done | bytes 8216
  0.7 0.0 copy-done.6
  0.7 0.0 copy-start
  0.7 0.9 %copy-done = bf16[2,1,6,4096]{3,0,2,1:T(2,128)(2,1)S(1)} copy-done((bf16[2,1,6,4096]{3,0,2,1:T(2,128)(2,1)S(1)}, bf16[2,1,6,4096]{3,0,2,1:T(2,128)(2,1)}, u32[]{:S(2)}) %copy-start) | copy-done | bytes 98328
  1.6 0.0 copy-start.1
  1.6 0.9 %copy-done.1 = bf16[5,1,2,2,128,16]{4,5,3,2,1,0:T(8,128)(2,1)S(1)} copy-done((bf16[5,1,2,2,128,16]{4,5,3,2,1,0:T(8,128)(2,1)S(1)}, bf16[5,1,2,2,128,16]{4,5,3,2,1,0:T(8,128)(2,1)}, u32[]{:S(2)}) %copy-start.1) | copy-done | bytes 81944
  2.5 0.0 copy-start.2
  2.5 0.7 %copy-done.2 = bf16[2,1,128,24]{2,3,1,0:T(8,128)(2,1)S(1)} copy-done((bf16[2,1,128,24]{2,3,1,0:T(8,128)(2,1)S(1)}, bf16[2,1,128,24]{2,3,1,0:T(8,128)(2,1)}, u32[]{:S(2)}) %copy-start.2) | copy-done | bytes 12312
  3.2 0.0 copy-start.4
  3.2 0.7 %copy-done.4 = s32[5,1,2,128]{3,2,1,0:T(2,128)S(1)} copy-done((s32[5,1,2,128]{3,2,1,0:T(2,128)S(1)}, s32[5,1,2,128]{3,2,1,0:T(2,128)}, u32[]{:S(2)}) %copy-start.4) | copy-done | bytes 5144
  3.9 0.0 copy-start.5
  3.9 0.7 %copy-done.5 = s32[5,1,2,128]{3,2,1,0:T(2,128)S(1)} copy-done((s32[5,1,2,128]{3,2,1,0:T(2,128)S(1)}, s32[5,1,2,128]{3,2,1,0:T(2,128)}, u32[]{:S(2)}) %copy-start.5) | copy-done | bytes 5144
  4.6 57.3 %aperture.1 = bf16[2,128,1024]{2,1,0:T(8,128)(2,1)S(1)} custom-call(bf16[6,2,4096]{2,1,0:T(2,128)(2,1)S(1)} %bitcast.17, bf16[2,2048]{1,0:T(2,128)(2,1)S(1)} %copy-done.3, bf16[2,24,128]{2,1,0:T(8,128)(2,1)S(1)} %bitcast.19, s32[1,24]{1,0:T(1,128)S(1)} %copy-done.6, bf16[20,16,128]{2,1,0:T(8,128)(2,1)S(1)} %bitcast.18, s32[5,2,128]{2,1,0:T(2,128)S(1)} %bitcast.20, ...), custom_call_target="tpu_custom_call" | custom-call | tf_op jit(solution)/shard_map/aperture/pallas_call | solution.py:370
  61.9 0.8 %copy.10 = bf16[2,128,1,1024]{3,1,2,0:T(8,128)(2,1)} copy(bf16[2,128,1,1024]{3,1,2,0:T(8,128)(2,1)S(1)} %bitcast.16) | data formatting | bytes 1048576
Async XLA Ops:
  0.0 0.7 %copy-start.3 = (bf16[2,2048]{1,0:T(2,128)(2,1)S(1)}, bf16[2,2048]{1,0:T(2,128)(2,1)}, u32[]{:S(2)}) copy-start(bf16[2,2048]{1,0:T(2,128)(2,1)} %chirp.1) | copy-start | bytes 24580
  0.0 0.7 %copy-start.6 = (s32[1,24]{1,0:T(1,128)S(1)}, s32[1,24]{1,0:T(1,128)}, u32[]{:S(2)}) copy-start(s32[1,24]{1,0:T(1,128)} %order.1) | copy-start | bytes 292
  0.7 0.9 %copy-start = (bf16[2,1,6,4096]{3,0,2,1:T(2,128)(2,1)S(1)}, bf16[2,1,6,4096]{3,0,2,1:T(2,128)(2,1)}, u32[]{:S(2)}) copy-start(bf16[2,1,6,4096]{3,0,2,1:T(2,128)(2,1)} %param.7) | copy-start | bytes 294916
  1.6 0.9 %copy-start.1 = (bf16[5,1,2,2,128,16]{4,5,3,2,1,0:T(8,128)(2,1)S(1)}, bf16[5,1,2,2,128,16]{4,5,3,2,1,0:T(8,128)(2,1)}, u32[]{:S(2)}) copy-start(bf16[5,1,2,2,128,16]{4,5,3,2,1,0:T(8,128)(2,1)} %param.11) | copy-start | bytes 245764
  2.5 0.7 %copy-start.2 = (bf16[2,1,128,24]{2,3,1,0:T(8,128)(2,1)S(1)}, bf16[2,1,128,24]{2,3,1,0:T(8,128)(2,1)}, u32[]{:S(2)}) copy-start(bf16[2,1,128,24]{2,3,1,0:T(8,128)(2,1)} %param.9) | copy-start | bytes 36868
  3.2 0.7 %copy-start.4 = (s32[5,1,2,128]{3,2,1,0:T(2,128)S(1)}, s32[5,1,2,128]{3,2,1,0:T(2,128)}, u32[]{:S(2)}) copy-start(s32[5,1,2,128]{3,2,1,0:T(2,128)} %param.12) | copy-start | bytes 15364
  3.9 0.7 %copy-start.5 = (s32[5,1,2,128]{3,2,1,0:T(2,128)S(1)}, s32[5,1,2,128]{3,2,1,0:T(2,128)}, u32[]{:S(2)}) copy-start(s32[5,1,2,128]{3,2,1,0:T(2,128)} %param.13) | copy-start | bytes 15364

commit v2 on v1

v2 whole, which is shorter than its diff:
```python
import functools

import jax
import jax.numpy as jnp
from jax import lax
from jax.experimental import pallas as pl
from jax.experimental.pallas import tpu as pltpu
from jax.sharding import PartitionSpec as P

F32 = jnp.float32
BF16 = jnp.bfloat16
MESH = pl.DeviceIdType.MESH

NX = 4
NY = 8
NZ = 4
NG = 4
PP = 6
PS = 24
RC = 4096
TAPS = 2048
CB = 128
QB = 128
SEC = 1024
NCH = 4
CW = SEC // NCH
BLK = 4 * PS


def staggered(chunks, lag):
    steps = [(2 * s + lag * c, c, s) for c in range(chunks) for s in range(5)]
    return [(c, s) for _, c, s in sorted(steps)]


ORDER = staggered(NCH, 1.5)


def dot(a, b):
    return jnp.dot(a, b, preferred_element_type=F32)


def dot_nt(a, b):
    return lax.dot_general(a, b, (((1,), (1,)), ((), ())), preferred_element_type=F32)


def flip(v, bit):
    return v + bit - 2 * bit * ((v // bit) % 2)


def one_hot(shape, dim0_of_dim1):
    rows = lax.broadcasted_iota(jnp.int32, shape, 0)
    cols = lax.broadcasted_iota(jnp.int32, shape, 1)
    return jnp.where(rows == dim0_of_dim1(cols), 1.0, 0.0).astype(BF16)


def kernel(
    echo_h, chirp_h, steer_h, order_h, coef_h, start_h, width_h, out,
    echo, chirp, steer, order, coef, start, width,
    halo, xf, x2, table, comp, recv, gath, pmat, zcoef, zstart, mats,
    tx0, tx1, tx2, tx3, ts, tt, tmat, psend, own, got,
    s_in, s_rim, r_rim, s_par, r_par, s_t, r_t, s_a, r_a, s_g, r_g, s_p, r_p,
):
    loads = []
    pairs = ((steer_h, steer), (order_h, order), (chirp_h, chirp), (coef_h, coef),
             (start_h, start), (width_h, width), (echo_h, echo))
    for i, (src, dst) in enumerate(pairs):
        loads.append(pltpu.make_async_copy(src, dst, s_in.at[i]))
        loads[-1].start()

    sec = lax.axis_index("section")
    sub = lax.axis_index("sub")
    rng = lax.axis_index("rng")
    y = sub % NY
    z = sub // NY
    base = z * NY

    def at_y(v):
        return {"sub": base + v}

    def at_z(v):
        return {"sub": v * NY + y}

    z1 = flip(z, 1)
    z2 = flip(z, 2)
    z3 = flip(z2, 1)
    y1 = flip(y, 1)
    y2 = flip(y, 2)
    y4 = flip(y, 4)
    up = (y + 1) % NY
    down = (y + NY - 1) % NY

    barrier = pltpu.get_barrier_semaphore()
    peers = [{"rng": (rng + 1) % NG}, {"rng": (rng + NG - 1) % NG}]
    for d in range(1, NX):
        other = (sec + d) % NX
        peers.append({"section": other})
        peers.append({"section": other, "sub": z2 * NY + y})
    peers += [at_z(z1), at_z(z2), at_z(z3), at_y(up), at_y(down), at_y(flip(y, 2)), at_y(y4)]
    for peer in peers:
        pl.semaphore_signal(barrier, inc=1, device_id=peer, device_id_type=MESH)
    for i in range(2):
        loads[i].wait()
    select = one_hot((PS, PS), lambda cols: order[...])
    eye32 = one_hot((32, PS), lambda cols: cols)
    sel_t = dot_nt(eye32, select).astype(BF16)
    ts[0:32, 0:QB] = dot(sel_t, steer[0]).astype(BF16)
    ts[0:32, QB:] = dot(sel_t, steer[1]).astype(BF16)

    loads[2].wait()
    wide = TAPS + 2 * CB
    for part in range(2):
        line = jnp.concatenate([chirp[part : part + 1, :].astype(F32), jnp.zeros((1, 2 * CB), F32)], axis=1)
        line = jnp.broadcast_to(line, (CB, wide))
        table[part * CB : (part + 1) * CB, :] = pltpu.roll(line, 0, 1, stride=1, stride_axis=0).astype(BF16)

    def load_rows(ref, blocks, first):
        lanes = blocks * CB
        for part in range(2):
            for p in range(PP):
                xf[part * 8 + p : part * 8 + p + 1, 0:lanes] = ref[p, part : part + 1, :].astype(F32)
            xf[part * 8 + PP : part * 8 + 8, 0:lanes] = jnp.zeros((8 - PP, lanes), F32)
        for b in range(blocks):
            tile = xf[:, b * CB : (b + 1) * CB]
            if ref is halo:
                tile = jnp.where(rng == NG - 1, jnp.zeros_like(tile), tile)
            tile = tile.astype(BF16)
            x2[first + b, :, 0:CB] = tile
            if first + b > 0:
                x2[first + b - 1, :, CB:] = tile

    nb = RC // CB
    nh = TAPS // CB

    def compress(first):
        rows = 16
        total = None
        for j in range(wide // (2 * CB)):
            lhs = x2[first + 2 * j : first + 2 * j + rows].reshape(rows * 16, 2 * CB)
            piece = dot_nt(lhs, table[:, 2 * j * CB : 2 * (j + 1) * CB])
            total = piece if total is None else total + piece
        for b in range(rows):
            re_rows = total[b * 16 : b * 16 + 8]
            im_rows = total[b * 16 + 8 : b * 16 + 16]
            re = re_rows[:, 0:CB] + im_rows[:, CB:]
            im = im_rows[:, 0:CB] - re_rows[:, CB:]
            at = (first + b) * CB
            comp[:, at : at + CB] = jnp.concatenate([re, im], axis=0).astype(BF16)

    loads[6].wait()
    load_rows(echo, nb, 0)
    compress(0)

    pl.semaphore_wait(barrier, len(peers))

    def send(src, dst, ssem, rsem, to):
        return pltpu.make_async_remote_copy(
            src_ref=src, dst_ref=dst, send_sem=ssem, recv_sem=rsem,
            device_id=to, device_id_type=MESH,
        )

    rim = send(echo_h.at[:, :, 0:TAPS], halo, s_rim, r_rim, {"rng": (rng + NG - 1) % NG})

    @pl.when(rng > 0)
    def _():
        rim.start()

    t0 = send(ts.at[0:32], tx0, s_t.at[0], r_t.at[0], at_y(y1))
    t0.start()

    def scatter(s):
        lanes = comp.at[:, s * SEC : (s + 1) * SEC]
        near = send(lanes, recv.at[0, sec], s_a.at[0, s], r_a.at[0, sec], {"section": s})
        far = send(lanes, recv.at[1, sec], s_a.at[1, s], r_a.at[1, sec], {"section": s, "sub": z2 * NY + y})
        far.start()

        @pl.when(sec != s)
        def _():
            near.start()

        return near, far

    sent = [scatter(0), scatter(1)]

    for i in range(3, 6):
        loads[i].wait()
    taps = lax.broadcasted_iota(jnp.int32, (16, QB), 0)
    for level in range(5):
        for side in range(2):
            keep = taps < width[level, side : side + 1, :]
            for part in range(2):
                i = level * 4 + side * 2 + part
                entry = jnp.where(keep, coef[i].astype(F32), 0.0)
                pmat[i] = entry.astype(BF16)
                if level >= 3:
                    zcoef[0, i - 12] = entry.astype(BF16)
            if level >= 3:
                zstart[0, (level - 3) * 2 + side : (level - 3) * 2 + side + 1, :] = start[level, side : side + 1, :]
    zstart[0, 4:8, :] = jnp.zeros((4, QB), jnp.int32)
    par = []
    for d, to, lo, hi in ((1, z1, 2, 8), (2, z2, 0, 2), (3, z3, 2, 4)):
        par.append(send(zcoef.at[0, lo:hi], zcoef.at[d, lo:hi], s_par.at[0, d], r_par.at[0, d], at_z(to)))
        par.append(send(zstart.at[0], zstart.at[d], s_par.at[1, d], r_par.at[1, d], at_z(to)))

    def band(slot, real, imag, first):
        offset = lax.broadcasted_iota(jnp.int32, (QB, QB), 0) - first
        re = jnp.zeros((QB, QB), F32)
        im = jnp.zeros((QB, QB), F32)
        for t in range(16):
            hit = offset == t
            re = jnp.where(hit, real[t : t + 1, :], re)
            im = jnp.where(hit, imag[t : t + 1, :], im)
        re_b = re.astype(BF16)
        mats[slot, 0:QB, 0:QB] = re_b
        mats[slot, QB:, QB:] = re_b
        mats[slot, 0:QB, QB:] = im.astype(BF16)
        mats[slot, QB:, 0:QB] = (-im).astype(BF16)

    def own_band(level, side):
        i = level * 4 + side * 2
        band(level * 2 + side, pmat[i].astype(F32), pmat[i + 1].astype(F32), start[level, side : side + 1, :])

    def far_band(slot, d, row):
        band(slot, zcoef[d, row * 2].astype(F32), zcoef[d, row * 2 + 1].astype(F32), zstart[d, row : row + 1, :])

    def grow(level, mine, theirs, rows):
        at_low = (y // (1 << level)) % 2 == 0
        a = dot(mine, mats[level * 2])[0:rows]
        b = dot(theirs, mats[level * 2 + 1])[0:rows]
        low = jnp.where(at_low, a, b)
        high = jnp.where(at_low, b, a)
        return jnp.concatenate([low, high], axis=0).astype(BF16)

    own_band(0, 0)
    own_band(0, 1)
    t0.wait()
    ts[32:80] = grow(0, ts[0:32], tx0[...], PS)
    t1 = send(ts.at[32:80], tx1, s_t.at[1], r_t.at[1], at_y(y2))
    t1.start()

    @pl.when(rng < NG - 1)
    def _():
        rim.wait_recv()

    load_rows(halo, nh, nb)
    x2[nb + nh - 1, :, CB:] = jnp.zeros((16, CB), BF16)
    compress(16)
    sent += [scatter(2), scatter(3)]
    recv[0, sec] = comp[:, pl.ds(pl.multiple_of(sec * SEC, SEC), SEC)]
    rows_i = lax.broadcasted_iota(jnp.int32, (BLK, 128), 0)
    cols_i = lax.broadcasted_iota(jnp.int32, (BLK, 128), 1)
    hot = jnp.zeros((BLK, 128), F32)
    for zz in range(2):
        for part in range(2):
            for x in range(NX):
                r0 = zz * 2 * PS + part * PS + x * PP
                c0 = zz * 64 + x * 16 + part * 8
                inside = (rows_i >= r0) & (rows_i < r0 + PP) & (cols_i - rows_i == c0 - r0)
                hot = jnp.where(inside, 1.0, hot)
    hot = hot.astype(BF16)
    own_band(1, 0)
    own_band(1, 1)
    t1.wait()
    ts[80:176] = grow(1, ts[32:80], tx1[...], 2 * PS)
    t2 = send(ts.at[80:176], tx2, s_t.at[2], r_t.at[2], at_y(y4))
    t2.start()

    for x in range(NX):
        for zz in range(2):
            arrival = send(comp.at[:, 0:SEC], recv.at[zz, x], s_a.at[zz, 0], r_a.at[zz, x], {"section": sec})
            if zz == 0:
                @pl.when(sec != x)
                def _():
                    arrival.wait_recv()
            else:
                arrival.wait_recv()
    for c in range(NCH):
        rows = recv[:, :, :, c * CW : (c + 1) * CW].reshape(2 * NX * 16, CW)
        gath[c, y] = dot(hot, rows).astype(BF16)

    def hop(direction, c, s):
        if direction == 0:
            at = (y + NY - s) % NY
            to = up
        else:
            at = (y + s) % NY
            to = down
        return send(gath.at[c, at], gath.at[c, at], s_g.at[direction, c, s], r_g.at[direction, c, s], at_y(to))

    def arrived(direction, c, s):
        if direction == 0:
            at = (y + 2 * NY - 1 - s) % NY
        else:
            at = (y + 1 + s) % NY
        return send(gath.at[c, at], gath.at[c, at], s_g.at[direction, c, s], r_g.at[direction, c, s], at_y(up))

    def legs(c, s):
        return (0, 1) if s < 3 else (c % 2,)

    def ring(c, s):
        for direction in legs(c, s):
            if s > 0:
                arrived(direction, c, s - 1).wait_recv()
            hop(direction, c, s).start()

    def settle(c):
        for direction in (0, 1):
            arrived(direction, c, 3 if direction in legs(c, 3) else 2).wait_recv()

    state = {}

    def part_a():
        for copy in par:
            copy.start()
        own_band(2, 0)
        own_band(2, 1)
        t2.wait()
        ts[176:368] = grow(2, ts[80:176], tx2[...], 4 * PS)
        state["t3"] = send(ts.at[176:368], tx3, s_t.at[3], r_t.at[3], at_z(z2))
        state["t3"].start()

    def part_b():
        for level in (3, 4):
            for side in range(2):
                own_band(level, side)

    def part_c():
        for copy in par:
            copy.wait()
        far_band(10, 1, 1)
        far_band(11, 1, 2)
        far_band(12, 1, 3)
        far_band(13, 2, 0)
        far_band(14, 3, 1)

    def chain(rows, first, second):
        return dot(dot(rows, mats[first]).astype(BF16), mats[second]).reshape(NY, PS, 2 * QB)

    def turned(rows):
        return jnp.concatenate([-rows[:, :, QB:], rows[:, :, 0:QB]], axis=2)

    eye = one_hot((2 * QB, 2 * QB), lambda cols: cols)

    def part_d():
        near_rows = ts[176:368]
        a0 = chain(near_rows, 6, 8)
        b0 = chain(near_rows, 10, 11)
        state["t3"].wait()
        far_rows = tx3[...]
        a1 = chain(far_rows, 13, 9)
        b1 = chain(far_rows, 14, 12)
        for i, (near_t, far_t) in enumerate(((a0, a1), (b0, b1))):
            full = jnp.concatenate([near_t, turned(near_t), far_t, turned(far_t)], axis=1)
            tt[...] = full.reshape(NY * BLK, 2 * QB).astype(BF16)
            tmat[i * 2 * QB : (i + 1) * 2 * QB, :] = dot_nt(eye, tt[...]).astype(BF16)

    swaps = []

    def image(c):
        settle(c)
        pulses = gath[c].reshape(NY * BLK, CW)
        psend[c] = dot(tmat[2 * QB :, :], pulses).reshape(2, QB, CW).astype(BF16)
        swap = send(psend.at[c], got.at[c], s_p.at[c], r_p.at[c], at_z(z1))
        swap.start()
        swaps.append(swap)
        own[c] = dot(tmat[0 : 2 * QB, :], pulses).reshape(2, QB, CW)

    parts = {NCH: part_a, NCH + NCH // 2: part_b, 2 * NCH: part_c, 2 * NCH + NCH // 2: part_d}
    for i, (c, s) in enumerate(ORDER):
        if s == 4:
            image(c)
        else:
            ring(c, s)
        if i + 1 in parts:
            parts[i + 1]()
    for (c, _), swap in zip([step for step in ORDER if step[1] == 4], swaps):
        swap.wait()
        out[:, :, c * CW : (c + 1) * CW] = (own[c] + got[c].astype(F32)).astype(BF16)
    for s, (near, far) in enumerate(sent):
        far.wait_send()

        @pl.when(sec != s)
        def _():
            near.wait_send()

    @pl.when(rng > 0)
    def _():
        rim.wait_send()

    for c in range(NCH):
        for s in range(4):
            for direction in legs(c, s):
                hop(direction, c, s).wait_send()


def on_device(echoes, chirp, steer, pulse_order, band_coef, band_start, band_width):
    echo = jnp.transpose(echoes[:, 0], (1, 0, 2))
    steer_t = jnp.swapaxes(steer[:, 0], 1, 2)
    coef = jnp.swapaxes(band_coef[:, 0], 3, 4).reshape(20, 16, QB)
    args = (echo, chirp, steer_t, pulse_order, coef, band_start[:, 0], band_width[:, 0])
    dma = pltpu.SemaphoreType.DMA
    vmem = pltpu.VMEM
    image = pl.pallas_call(
        kernel,
        out_shape=jax.ShapeDtypeStruct((2, QB, SEC), BF16),
        in_specs=[pl.BlockSpec(memory_space=pltpu.HBM)] * 7,
        out_specs=pl.BlockSpec(memory_space=pltpu.VMEM),
        scratch_shapes=[
            vmem((PP, 2, RC), BF16),
            vmem((2, TAPS), BF16),
            vmem((2, PS, QB), BF16),
            vmem((1, PS), jnp.int32),
            vmem((20, 16, QB), BF16),
            vmem((5, 2, QB), jnp.int32),
            vmem((5, 2, QB), jnp.int32),
            vmem((PP, 2, TAPS), BF16),
            vmem((16, RC), F32),
            vmem((48, 16, 2 * CB), BF16),
            vmem((2 * CB, TAPS + 2 * CB), BF16),
            vmem((16, RC), BF16),
            vmem((2, NX, 16, SEC), BF16),
            vmem((NCH, NY, BLK, CW), BF16),
            vmem((20, 16, QB), BF16),
            vmem((4, 8, 16, QB), BF16),
            vmem((4, 8, QB), jnp.int32),
            vmem((15, 2 * QB, 2 * QB), BF16),
            vmem((32, 2 * QB), BF16),
            vmem((2 * PS, 2 * QB), BF16),
            vmem((4 * PS, 2 * QB), BF16),
            vmem((8 * PS, 2 * QB), BF16),
            vmem((368, 2 * QB), BF16),
            vmem((NY * BLK, 2 * QB), BF16),
            vmem((4 * QB, NY * BLK), BF16),
            vmem((NCH, 2, QB, CW), BF16),
            vmem((NCH, 2, QB, CW), F32),
            vmem((NCH, 2, QB, CW), BF16),
            dma((7,)),
            dma, dma,
            dma((2, 4)), dma((2, 4)),
            dma((4,)), dma((4,)),
            dma((2, NX)), dma((2, NX)),
            dma((2, NCH, 4)), dma((2, NCH, 4)),
            dma((NCH,)), dma((NCH,)),
        ],
        compiler_params=pltpu.CompilerParams(
            collective_id=0, has_side_effects=True, vmem_limit_bytes=40 << 20
        ),
        name="aperture",
    )(*(pltpu.with_memory_space_constraint(arg, pltpu.HBM) for arg in args))
    return image[:, :, None, :]


def solution(mesh):
    return jax.shard_map(
        on_device,
        mesh=mesh,
        in_specs=(
            P(None, "sub", "section", "rng"),
            P(),
            P(None, "sub", None, None),
            P("sub", None),
            P(None, "sub", None, None, None, None),
            P(None, "sub", None, None),
            P(None, "sub", None, None),
        ),
        out_specs=P(None, "sub", "rng", "section"),
        check_vma=False,
    )
```

time: 63.1 us -> 53 us (0.84)
  Pallas kernels: 57.3 us -> 51.8 us
  local copies, waits for them, and re-layouts: 5.36 us -> 0.8 us
    pallas_call x1, Pallas kernels: 57.3 us -> 51.8 us  [on_device(): pl.pallas_call(kernel, out_shape=jax.ShapeDtypeStruct((2, QB, SEC), BF16)...]
    unnamed x15 -> x1, local copies, waits for them, and re-layouts: 5.36 us -> 0.8 us
where the time goes in v2:
time: 53 us; the launch traced here: 52.6 us
  Pallas kernels  51.8 us (98%)
  local copies, waits for them, and re-layouts  0.8 us (2%)
    pallas_call x1, Pallas kernels, on_device(): pl.pallas_call(kernel, out_shape=jax.ShapeDtypeStruct((2, QB, SEC), BF16)...  51.8 us

profile of v2, /device:TPU:6, one launch (start us, length us, event | category | flops | bytes accessed | tf_op | source)
XLA Modules:
  0.0 52.6 jit_solution(13924600345422374929)
XLA Ops:
  0.0 51.8 %aperture.1 = bf16[2,128,1024]{2,1,0:T(8,128)(2,1)S(1)} custom-call(bf16[6,2,4096]{2,1,0:T(2,128)(2,1)} %bitcast.17, bf16[2,2048]{1,0:T(2,128)(2,1)} %chirp_h.1, bf16[2,24,128]{2,1,0:T(8,128)(2,1)} %bitcast.19, s32[1,24]{1,0:T(1,128)} %order_h.1, bf16[20,16,128]{2,1,0:T(8,128)(2,1)} %bitcast.18, s32[5,2,128]{2,1,0:T(2,128)} %bitcast.20, s32[5,2,128]{2,1,0:T(2,128)} %bitcast.21), custom_call_target="tpu_custom_call" | custom-call | tf_op jit(solution)/shard_map/aperture/pallas_call | solution.py:402
  51.8 0.8 %copy.10 = bf16[2,128,1,1024]{3,1,2,0:T(8,128)(2,1)} copy(bf16[2,128,1,1024]{3,1,2,0:T(8,128)(2,1)S(1)} %bitcast.16) | data formatting | bytes 1048576

commit v3 on v2

--- a/solution.py
+++ b/solution.py
@@ -22,7 +22,7 @@
 CB = 128
 QB = 128
 SEC = 1024
-NCH = 4
+NCH = 8
 CW = SEC // NCH
 BLK = 4 * PS
 
@@ -32,7 +32,7 @@
     return [(c, s) for _, c, s in sorted(steps)]
 
 
-ORDER = staggered(NCH, 1.5)
+ORDER = staggered(NCH, 0.7)
 
 
 def dot(a, b):

time: 53 us -> 52 us (0.981)
  Pallas kernels: 51.8 us -> 51 us
    pallas_call x1, Pallas kernels: 51.8 us -> 51 us  [on_device(): pl.pallas_call(kernel, out_shape=jax.ShapeDtypeStruct((2, QB, SEC), BF16)...]
where the time goes in v3:
time: 52 us; the launch traced here: 51.8 us
  Pallas kernels  51 us (98%)
  local copies, waits for them, and re-layouts  0.8 us (2%)
    pallas_call x1, Pallas kernels, on_device(): pl.pallas_call(kernel, out_shape=jax.ShapeDtypeStruct((2, QB, SEC), BF16)...  51 us

profile of v3, /device:TPU:6, one launch (start us, length us, event | category | flops | bytes accessed | tf_op | source)
XLA Modules:
  0.0 51.8 jit_solution(767581639060239567)
XLA Ops:
  0.0 51.0 %aperture.1 = bf16[2,128,1024]{2,1,0:T(8,128)(2,1)S(1)} custom-call(bf16[6,2,4096]{2,1,0:T(2,128)(2,1)} %bitcast.17, bf16[2,2048]{1,0:T(2,128)(2,1)} %chirp_h.1, bf16[2,24,128]{2,1,0:T(8,128)(2,1)} %bitcast.19, s32[1,24]{1,0:T(1,128)} %order_h.1, bf16[20,16,128]{2,1,0:T(8,128)(2,1)} %bitcast.18, s32[5,2,128]{2,1,0:T(2,128)} %bitcast.20, s32[5,2,128]{2,1,0:T(2,128)} %bitcast.21), custom_call_target="tpu_custom_call" | custom-call | tf_op jit(solution)/shard_map/aperture/pallas_call | solution.py:402
  51.0 0.8 %copy.10 = bf16[2,128,1,1024]{3,1,2,0:T(8,128)(2,1)} copy(bf16[2,128,1,1024]{3,1,2,0:T(8,128)(2,1)S(1)} %bitcast.16) | data formatting | bytes 1048576

commit v4 on v3

--- a/solution.py
+++ b/solution.py
@@ -297,7 +297,7 @@
         return (0, 1) if s < 3 else (c % 2,)
 
     def ring(c, s):
-        for direction in legs(c, s):
+        for direction in legs(c, s)[:: 1 if c % 2 else -1]:
             if s > 0:
                 arrived(direction, c, s - 1).wait_recv()
             hop(direction, c, s).start()

time: 52 us -> 52.3 us (level)
  no operation moved by 1% of the time
where the time goes in v4:
time: 52.3 us; the launch traced here: 52.2 us
  Pallas kernels  51.3 us (98%)
  local copies, waits for them, and re-layouts  0.8 us (2%)
    pallas_call x1, Pallas kernels, on_device(): pl.pallas_call(kernel, out_shape=jax.ShapeDtypeStruct((2, QB, SEC), BF16)...  51.3 us

profile of v4, /device:TPU:6, one launch (start us, length us, event | category | flops | bytes accessed | tf_op | source)
XLA Modules:
  0.0 52.2 jit_solution(12851889331225712426)
XLA Ops:
  0.0 51.3 %aperture.1 = bf16[2,128,1024]{2,1,0:T(8,128)(2,1)S(1)} custom-call(bf16[6,2,4096]{2,1,0:T(2,128)(2,1)} %bitcast.17, bf16[2,2048]{1,0:T(2,128)(2,1)} %chirp_h.1, bf16[2,24,128]{2,1,0:T(8,128)(2,1)} %bitcast.19, s32[1,24]{1,0:T(1,128)} %order_h.1, bf16[20,16,128]{2,1,0:T(8,128)(2,1)} %bitcast.18, s32[5,2,128]{2,1,0:T(2,128)} %bitcast.20, s32[5,2,128]{2,1,0:T(2,128)} %bitcast.21), custom_call_target="tpu_custom_call" | custom-call | tf_op jit(solution)/shard_map/aperture/pallas_call | solution.py:402
  51.4 0.8 %copy.10 = bf16[2,128,1,1024]{3,1,2,0:T(8,128)(2,1)} copy(bf16[2,128,1,1024]{3,1,2,0:T(8,128)(2,1)S(1)} %bitcast.16) | data formatting | bytes 1048576
